TPU v7x, 32 devices: a whole 2x2x4 slice. The times are simulated.
32 devices in a mesh: groups: 2 (over x), tensor: 4 (over y, core), dp: 4 (over z).
Axes of the slice: x: 2, y: 2, z: 4, core: 2. Of those that a mesh axis runs over, the one named last changes fastest.
Arguments:
- hidden_in: bfloat16 [1024, 8192], P(('groups', 'dp'), 'tensor'), parts along dimension 0, may hold values from -6 to 6
- out_grad: bfloat16 [1024, 8192], P(('groups', 'dp'), 'tensor'), parts along dimension 0, may hold values from -6 to 6
- w_gate_up: bfloat16 [2, 28672, 8192], P(None, ('tensor', 'dp')), may hold values from -0.0625 to 0.0625
- w_down: bfloat16 [28672, 8192], P(('tensor', 'dp')), may hold values from -0.03125 to 0.03125
- feat_proj: bfloat16 [8192, 192], P('tensor'), may hold values from -0.0625 to 0.0625
- unit_proj: bfloat16 [28672, 192], P(('tensor', 'dp')), may hold values from -0.03125 to 0.03125
- precond: float32 [3, 4096, 4096], P(None, ('tensor', 'dp')), may hold values from -20 to 20
Outputs:
- precond_grad: float32 [3, 8, 4096], P(None, 'groups', ('tensor', 'dp')), parts along dimension 1
There are 2 independent parts, one for each index of `groups`. A program takes and returns all parts, laid end to end along the dimension named above; an argument that names none is the same for every part. Nothing has to cross between parts.
All inputs are finite; a program needn't handle non-finite values.
Results may differ from a plain program's by a relative error of at most 0.0029.
Values may be sent and summed in bfloat16 or wider, within the bound.
No kernel may reach another device: no remote copies, remote signals or barrier semaphores. Data moves between devices by JAX's collectives and lax.ppermute only.
A program may use at most 256 MiB of HBM per device.

v0:
```python
import jax
import jax.numpy as jnp
from jax import lax
from jax.sharding import PartitionSpec as P

K = 64
SEQ = 128
contract_last = (((1,), (1,)), ((), ()))


def project_pair(rows_in, rows_out, columns):
    return jnp.concatenate(
        [
            jnp.dot(rows_in, columns[:, : 2 * K], preferred_element_type=jnp.float32),
            jnp.dot(rows_out, columns[:, 2 * K :], preferred_element_type=jnp.float32),
        ],
        axis=1,
    )


def form_sketch(in_side, out_side):
    seq_count = in_side.shape[0] // SEQ
    left_rows = in_side.reshape(seq_count, SEQ, 3, K)
    right_rows = out_side.reshape(seq_count, SEQ, 3, K)
    sketch = jnp.einsum("stwi,stwj->wsij", left_rows, right_rows, precision=lax.Precision.HIGHEST)
    sketch = sketch * SEQ ** (-0.5)
    return sketch.reshape(3, seq_count, K * K)


def local(hidden_in, out_grad, w_gate_up, w_down, feat_proj, unit_proj, precond):
    unit_width = w_down.shape[0]
    model_width = w_down.shape[1]
    w_both = w_gate_up.reshape(2 * unit_width, model_width)
    paired = jnp.stack([hidden_in, out_grad])
    tokens = hidden_in.shape[0] * lax.axis_size("dp")
    columns = lax.all_gather(feat_proj, "tensor", axis=0, tiled=True)
    feat_side = None
    rows_all = lax.all_gather(paired, "dp", axis=1, tiled=True)
    initial = [
        jnp.zeros((tokens, 2 * unit_width), jnp.float32),
        jnp.zeros((tokens, unit_width), jnp.float32),
    ]
    initial.append(jnp.zeros((tokens, 3 * K), jnp.float32))
    pieces = lax.all_gather(rows_all, "tensor", axis=2, tiled=True)
    result = [
        lax.dot_general(pieces[0], w_both, contract_last, preferred_element_type=jnp.float32),
        lax.dot_general(pieces[1], w_down, contract_last, preferred_element_type=jnp.float32),
    ]
    result.append(project_pair(pieces[0], pieces[1], columns))
    folded = tuple(result)
    pre_act = folded[0]
    hid_grad = folded[1]
    feat_side = folded[2]
    gate_pre = pre_act[:, :unit_width]
    up_pre = pre_act[:, unit_width:]
    gate_sig = jax.nn.sigmoid(gate_pre)
    silu_gate = gate_pre * gate_sig
    hidden = (silu_gate * up_pre).astype(jnp.bfloat16)
    gate_grad = (hid_grad * up_pre * gate_sig * (1.0 + gate_pre * (1.0 - gate_sig))).astype(
        jnp.bfloat16
    )
    up_grad = (hid_grad * silu_gate).astype(jnp.bfloat16)
    unit_part = jnp.concatenate(
        [
            jnp.dot(gate_grad, unit_proj[:, :K], preferred_element_type=jnp.float32),
            jnp.dot(up_grad, unit_proj[:, K : 2 * K], preferred_element_type=jnp.float32),
            jnp.dot(hidden, unit_proj[:, 2 * K :], preferred_element_type=jnp.float32),
        ],
        axis=1,
    )
    unit_side = lax.psum(unit_part, ("tensor", "dp"))
    in_side = jnp.concatenate([feat_side[:, : 2 * K], unit_side[:, 2 * K :]], axis=1)
    out_side = jnp.concatenate([unit_side[:, : 2 * K], feat_side[:, 2 * K :]], axis=1)
    sketch = form_sketch(in_side, out_side)
    return jnp.einsum("wrc,wsc->wsr", precond, sketch, precision=lax.Precision.HIGHEST)


def solution(mesh):
    in_specs = (
        P(("groups", "dp"), "tensor"),
        P(("groups", "dp"), "tensor"),
        P(None, ("tensor", "dp"), None),
        P(("tensor", "dp"), None),
        P("tensor", None),
        P(("tensor", "dp"), None),
        P(None, ("tensor", "dp"), None),
    )
    out_specs = P(None, "groups", ("tensor", "dp"))
    return jax.shard_map(local, mesh=mesh, in_specs=in_specs, out_specs=out_specs, check_vma=False)
```

profile of v0, /device:TPU:0, one launch (start us, length us, event | category | flops | bytes accessed | tf_op | source)
XLA Modules:
  0.0 386.8 jit_solution(336281864798562320)
XLA Ops:
  6.5 0.0 all-gather.4.cloned.1.call-start
  6.5 2.3 pad_maximum_fusion
  8.8 0.0 all-gather.4.cloned.1.call-update
  8.8 0.0 all-gather.6.cloned.1.call-start
  8.9 83.6 %all-gather.4.cloned.1.call-done = bf16[2,512,2048]{2,1,0:T(8,128)(2,1)} async-done(((bf16[2,128,2048]{2,1,0:T(8,128)(2,1)}), bf16[2,512,2048]{2,1,0:T(8,128)(2,1)}) %all-gather.4.cloned.1.call-update) | async-done | bytes 4194320 | tf_op jit(solution)/shard_map/all_gather | solution.py:38
  92.4 0.0 all-gather.6.cloned.1.call-update
  92.5 0.0 all-gather.8.cloned.1.call-start
  92.5 0.7 all-gather.8.cloned.1.call-update
  93.2 0.0 all-reduce.2.cloned.1.call-start
  93.3 105.2 %all-gather.6.cloned.1.call-done = bf16[2,512,8192]{2,1,0:T(8,128)(2,1)} async-done(((bf16[2,512,2048]{2,1,0:T(8,128)(2,1)}), bf16[2,512,8192]{2,1,0:T(8,128)(2,1)}) %all-gather.6.cloned.1.call-update) | async-done | bytes 16777232 | tf_op jit(solution)/shard_map/all_gather | solution.py:44
  198.5 0.0 copy-start
  198.5 38.6 %fusion = f32[512,3584]{1,0:T(8,128)} fusion(bf16[3584,8192]{1,0:T(8,128)(2,1)} %bitcast.23, bf16[2,512,8192]{2,1,0:T(8,128)(2,1)} %all-gather.6.cloned.1.call-done), kind=kOutput, calls=%fused_computation.2 | convolution fusion | flops 30064771072 | bytes 74448896 | tf_op jit(solution)/shard_map/dot_general | solution.py:46
  237.1 0.0 copy-done
  237.1 4.3 %fusion.7 = f32[512,64]{0,1:T(8,128)S(1)} fusion(f32[512,3584]{1,0:T(8,128)} %fusion, bf16[1792,192]{0,1:T(8,128)(2,1)S(1)} %copy-done), kind=kOutput, calls=%fused_computation.13 | convolution fusion | flops 122945536 | bytes 7700480 | tf_op jit(solution)/shard_map/dot_general | solution.py:67
  241.3 22.9 %fusion.3 = f32[512,1792]{1,0:T(8,128)} fusion(bf16[1792,8192]{1,0:T(8,128)(2,1)} %param.10, bf16[2,512,8192]{2,1,0:T(8,128)(2,1)} %all-gather.6.cloned.1.call-done), kind=kOutput, calls=%fused_computation.5 | convolution fusion | flops 15032385536 | bytes 41418752 | tf_op jit(solution)/shard_map/dot_general | solution.py:47
  264.3 0.0 copy-start.1
  264.3 0.0 copy-start.2
  264.3 4.4 %fusion.6 = f32[512,64]{0,1:T(8,128)S(1)} fusion(f32[512,1792]{1,0:T(8,128)} %fusion.3, f32[512,3584]{1,0:T(8,128)} %fusion, bf16[1792,192]{0,1:T(8,128)(2,1)S(1)} %copy-done), kind=kOutput, calls=%fused_computation.12 | convolution fusion | flops 122945536 | bytes 7700480 | tf_op jit(solution)/shard_map/dot_general | solution.py:66
  268.7 0.8 copy-done.1
  269.5 1.0 copy-done.2
  270.5 1.6 fusion.8
  272.1 0.8 pad_maximum_fusion.1
  272.9 0.0 all-reduce.2.cloned.1.call-update
  272.9 0.0 all-gather.8.cloned.1.call-done
  272.9 6.9 %fusion.1 = f32[512,128]{0,1:T(8,128)S(1)} fusion(bf16[2,512,8192]{2,1,0:T(8,128)(2,1)} %all-gather.6.cloned.1.call-done, bf16[8192,192]{0,1:T(8,128)(2,1)} %all-gather.8.cloned.1.call-done), kind=kOutput, calls=%fused_computation.3 | convolution fusion | flops 1073741824 | bytes 10747904 | tf_op jit(solution)/shard_map/dot_general | solution.py:14
  279.8 6.3 %fusion.2 = f32[512,64]{0,1:T(8,128)S(1)} fusion(bf16[2,512,8192]{2,1,0:T(8,128)(2,1)} %all-gather.6.cloned.1.call-done, bf16[8192,192]{0,1:T(8,128)(2,1)} %all-gather.8.cloned.1.call-done), kind=kOutput, calls=%fused_computation.4 | convolution fusion | flops 536870912 | bytes 9568256 | tf_op jit(solution)/shard_map/dot_general | solution.py:15
  286.1 77.3 %all-reduce.2.cloned.1.call-done = f32[512,192]{0,1:T(8,128)} async-done(((f32[512,192]{0,1:T(8,128)}), f32[512,192]{0,1:T(8,128)}) %all-reduce.2.cloned.1.call-update) | async-done | bytes 393232 | tf_op jit(solution)/shard_map/psum | solution.py:71
  363.4 0.9 slice.51
  364.4 0.1 reshape.13
  364.5 1.0 slice.52
  365.5 0.1 reshape.14
  365.7 0.8 convolution_multiply_fusion
  366.4 0.2 reshape.15
  366.6 13.6 %fusion.20 = f32[3,4,256]{2,1,0:T(4,128)} fusion(f32[3,4,4096]{2,1,0:T(4,128)S(1)} %reshape.15, f32[3,256,4096]{2,1,0:T(8,128)} %param.13), kind=kOutput, calls=%fused_computation.29 | convolution fusion | flops 150994944 | bytes 12791808 | tf_op jit(solution)/shard_map/wrc,wsc->wsr/dot_general | solution.py:75
  (2 shorter events, 0.1 us)
Async XLA Ops:
  6.5 85.9 %all-gather.4.cloned.1.call-start = ((), (), s32[]{:S(2)}) async-start(), calls=%async_computation | async-start | bytes 5242880 | tf_op jit(solution)/shard_map/all_gather | solution.py:38
  8.8 189.7 %all-gather.6.cloned.1.call-start = ((), (), s32[]{:S(2)}) async-start(), calls=%async_computation.1 | async-start | bytes 20971520 | tf_op jit(solution)/shard_map/all_gather | solution.py:44
  92.5 180.4 %all-gather.8.cloned.1.call-start = ((), (), s32[]{:S(2)}) async-start(), calls=%async_computation.2 | async-start | bytes 3932160 | tf_op jit(solution)/shard_map/all_gather | solution.py:36
  93.2 270.2 %all-reduce.2.cloned.1.call-start = ((), (), s32[]{:S(2)}) async-start(), calls=%async_computation.3 | async-start | bytes 786432 | tf_op jit(solution)/shard_map/psum | solution.py:71
  198.5 38.6 %copy-start = (bf16[1792,192]{0,1:T(8,128)(2,1)S(1)}, bf16[1792,192]{0,1:T(8,128)(2,1)}, u32[]{:S(2)}) copy-start(bf16[1792,192]{0,1:T(8,128)(2,1)} %param.12) | copy-start | bytes 2064388
  264.3 5.2 %copy-start.1 = (f32[512,3584]{1,0:T(8,128)S(1)}, f32[512,3584]{1,0:T(8,128)}, u32[]{:S(2)}) copy-start(f32[512,3584]{1,0:T(8,128)} %fusion) | copy-start | bytes 22020100
  264.3 6.3 %copy-start.2 = (f32[512,1792]{1,0:T(8,128)S(1)}, f32[512,1792]{1,0:T(8,128)}, u32[]{:S(2)}) copy-start(f32[512,1792]{1,0:T(8,128)} %fusion.3) | copy-start | bytes 11010052
Sparse Core Ops, SparseCore 0:
  9.0 83.4 all-gather.3
  94.0 104.4 all-gather.5
  200.1 28.5 all-gather.7
  273.0 90.3 all-reduce.1
where the time goes:
time: 387 us
  waiting for transfers between devices  267 us (69%)
  matrix products  99.3 us (26%)
  between operations  13.2 us (3%)
  local copies, waits for them, and re-layouts  4.2 us (1%)
    all_gather x1, waiting for transfers between devices, local(): pieces = lax.all_gather(rows_all, 'tensor', axis=2, tiled=True)  105 us
    all_gather x1, waiting for transfers between devices, local(): rows_all = lax.all_gather(paired, 'dp', axis=1, tiled=True)  83.6 us
    psum x1, waiting for transfers between devices, local(): unit_side = lax.psum(unit_part, ('tensor', 'dp'))  77.3 us
    dot_general x1, matrix products, local(): lax.dot_general(pieces[0], w_both, contract_last, preferred_element_type=...  38.6 us
    dot_general x1, matrix products, local(): lax.dot_general(pieces[1], w_down, contract_last, preferred_element_type=...  22.9 us
    dot_general x1, matrix products, local(): jnp.einsum('wrc,wsc->wsr', precond, sketch, precision=lax.Precision.HIGHEST)  13.6 us
  transfers between devices with their start and end apart: 4, of which 3 were waited for; matrix products, arithmetic and copies ran while one was open for 22% of the time, Pallas kernels for 0%

commit v1 on v0

--- a/solution.py
+++ b/solution.py
@@ -68,7 +68,7 @@
         ],
         axis=1,
     )
-    unit_side = lax.psum(unit_part, ("tensor", "dp"))
+    unit_side = jnp.sum(lax.all_gather(unit_part, ("tensor", "dp")), axis=0)
     in_side = jnp.concatenate([feat_side[:, : 2 * K], unit_side[:, 2 * K :]], axis=1)
     out_side = jnp.concatenate([unit_side[:, : 2 * K], feat_side[:, 2 * K :]], axis=1)
     sketch = form_sketch(in_side, out_side)

time: 387 us -> 367 us (0.948)
  waiting for transfers between devices: 267 us -> 239 us
  local copies, waits for them, and re-layouts: 4.2 us -> 10.8 us
    psum x1 -> x0, waiting for transfers between devices: 77.3 us -> none  [local(): unit_side = lax.psum(unit_part, ('tensor', 'dp'))]
    all_gather x0 -> x1, waiting for transfers between devices: none -> 49 us  [local(): unit_side = jnp.sum(lax.all_gather(unit_part, ('tensor', 'dp')), axis=0)]
    unnamed x6 -> x9, local copies, waits for them, and re-layouts: 1.86 us -> 10.3 us
  transfers between devices with their start and end apart: 4 -> 4, of which waited for: 3 -> 3; matrix products, arithmetic and copies ran while one was open for 22% -> 23% of each run, Pallas kernels for 0% -> 0%
where the time goes in v1:
time: 367 us; the launch traced here: 366 us
  waiting for transfers between devices  239 us (65%)
  matrix products  99.2 us (27%)
  between operations  13.2 us (4%)
  local copies, waits for them, and re-layouts  10.8 us (3%)
  other arithmetic  4.54 us (1%)
    all_gather x1, waiting for transfers between devices, local(): pieces = lax.all_gather(rows_all, 'tensor', axis=2, tiled=True)  105 us
    all_gather x1, waiting for transfers between devices, local(): rows_all = lax.all_gather(paired, 'dp', axis=1, tiled=True)  83.6 us
    all_gather x1, waiting for transfers between devices, local(): unit_side = jnp.sum(lax.all_gather(unit_part, ('tensor', 'dp')), axis=0)  49 us
    dot_general x1, matrix products, local(): lax.dot_general(pieces[0], w_both, contract_last, preferred_element_type=...  38.6 us
    dot_general x1, matrix products, local(): lax.dot_general(pieces[1], w_down, contract_last, preferred_element_type=...  22.9 us
    dot_general x1, matrix products, local(): jnp.einsum('wrc,wsc->wsr', precond, sketch, precision=lax.Precision.HIGHEST)  13.6 us
    unnamed x9, local copies, waits for them, and re-layouts  10.3 us
  transfers between devices with their start and end apart: 4, of which 3 were waited for; matrix products, arithmetic and copies ran while one was open for 23% of the time, Pallas kernels for 0%

profile of v1, /device:TPU:0, one launch (start us, length us, event | category | flops | bytes accessed | tf_op | source)
XLA Modules:
  0.0 366.3 jit_solution(184224654995826279)
XLA Ops:
  6.5 0.0 all-gather.6.cloned.1.call-start
  6.5 2.3 pad_maximum_fusion
  8.8 0.0 all-gather.6.cloned.1.call-update
  8.8 0.0 all-gather.8.cloned.1.call-start
  8.9 83.6 %all-gather.6.cloned.1.call-done = bf16[2,512,2048]{2,1,0:T(8,128)(2,1)} async-done(((bf16[2,128,2048]{2,1,0:T(8,128)(2,1)}), bf16[2,512,2048]{2,1,0:T(8,128)(2,1)}) %all-gather.6.cloned.1.call-update) | async-done | bytes 4194320 | tf_op jit(solution)/shard_map/all_gather | solution.py:38
  92.4 0.0 all-gather.8.cloned.1.call-update
  92.5 0.0 all-gather.10.cloned.1.call-start
  92.5 0.7 all-gather.10.cloned.1.call-update
  93.2 0.0 all-gather.12.cloned.1.call-start
  93.3 105.2 %all-gather.8.cloned.1.call-done = bf16[2,512,8192]{2,1,0:T(8,128)(2,1)} async-done(((bf16[2,512,2048]{2,1,0:T(8,128)(2,1)}), bf16[2,512,8192]{2,1,0:T(8,128)(2,1)}) %all-gather.8.cloned.1.call-update) | async-done | bytes 16777232 | tf_op jit(solution)/shard_map/all_gather | solution.py:44
  198.5 0.0 copy-start.1
  198.5 38.6 %fusion = f32[512,3584]{1,0:T(8,128)} fusion(bf16[3584,8192]{1,0:T(8,128)(2,1)} %bitcast.29, bf16[2,512,8192]{2,1,0:T(8,128)(2,1)} %all-gather.8.cloned.1.call-done), kind=kOutput, calls=%fused_computation.2 | convolution fusion | flops 30064771072 | bytes 74448896 | tf_op jit(solution)/shard_map/dot_general | solution.py:46
  237.1 0.0 copy-done.1
  237.1 4.3 %fusion.7 = f32[512,64]{0,1:T(8,128)S(1)} fusion(f32[512,3584]{1,0:T(8,128)} %fusion, bf16[1792,192]{0,1:T(8,128)(2,1)S(1)} %copy-done.1), kind=kOutput, calls=%fused_computation.14 | convolution fusion | flops 122945536 | bytes 7700480 | tf_op jit(solution)/shard_map/dot_general | solution.py:67
  241.3 22.9 %fusion.3 = f32[512,1792]{1,0:T(8,128)} fusion(bf16[1792,8192]{1,0:T(8,128)(2,1)} %param.10, bf16[2,512,8192]{2,1,0:T(8,128)(2,1)} %all-gather.8.cloned.1.call-done), kind=kOutput, calls=%fused_computation.5 | convolution fusion | flops 15032385536 | bytes 41418752 | tf_op jit(solution)/shard_map/dot_general | solution.py:47
  264.2 0.0 copy-start.2
  264.2 0.0 copy-start.3
  264.2 4.4 %fusion.6 = f32[512,64]{0,1:T(8,128)S(1)} fusion(f32[512,1792]{1,0:T(8,128)} %fusion.3, f32[512,3584]{1,0:T(8,128)} %fusion, bf16[1792,192]{0,1:T(8,128)(2,1)S(1)} %copy-done.1), kind=kOutput, calls=%fused_computation.13 | convolution fusion | flops 122945536 | bytes 7700480 | tf_op jit(solution)/shard_map/dot_general | solution.py:66
  268.6 0.8 copy-done.2
  269.5 1.0 copy-done.3
  270.5 1.6 fusion.8
  272.1 0.8 pad_maximum_fusion.1
  272.9 0.0 all-gather.12.cloned.1.call-update
  272.9 0.0 all-gather.10.cloned.1.call-done
  272.9 0.0 copy-start
  272.9 6.4 %fusion.2 = f32[512,64]{0,1:T(8,128)S(1)} fusion(bf16[2,512,8192]{2,1,0:T(8,128)(2,1)} %all-gather.8.cloned.1.call-done, bf16[8192,192]{0,1:T(8,128)(2,1)} %all-gather.10.cloned.1.call-done), kind=kOutput, calls=%fused_computation.4 | convolution fusion | flops 536870912 | bytes 9568256 | tf_op jit(solution)/shard_map/dot_general | solution.py:15
  279.3 0.0 copy-done
  279.3 6.7 %fusion.1 = f32[512,128]{0,1:T(8,128)S(1)} fusion(bf16[2,512,8192]{2,1,0:T(8,128)(2,1)} %all-gather.8.cloned.1.call-done, bf16[8192,192]{0,1:T(8,128)(2,1)S(1)} %copy-done), kind=kOutput, calls=%fused_computation.3 | convolution fusion | flops 1073741824 | bytes 10747904 | tf_op jit(solution)/shard_map/dot_general | solution.py:14
  286.0 49.0 %all-gather.12.cloned.1.call-done = f32[8192,192]{0,1:T(8,128)} async-done(((f32[512,192]{0,1:T(8,128)}), f32[8192,192]{0,1:T(8,128)}) %all-gather.12.cloned.1.call-update) | async-done | bytes 6291472 | tf_op jit(solution)/shard_map/all_gather | solution.py:71
  335.0 8.4 %copy.10 = f32[24,8,16,512]{3,2,1,0:T(8,128)S(1)} copy(f32[24,8,16,512]{3,1,2,0:T(8,128)} %bitcast.26) | data formatting | bytes 12582912
  343.4 1.4 bitcast_reduce_fusion
  344.9 0.1 reshape.14
  345.1 0.1 reshape.13
  345.2 0.8 convolution_multiply_fusion
  346.0 0.2 reshape.15
  346.2 13.6 %fusion.20 = f32[3,4,256]{2,1,0:T(4,128)} fusion(f32[3,4,4096]{2,1,0:T(4,128)S(1)} %reshape.15, f32[3,256,4096]{2,1,0:T(8,128)} %param.13), kind=kOutput, calls=%fused_computation.30 | convolution fusion | flops 150994944 | bytes 12791808 | tf_op jit(solution)/shard_map/wrc,wsc->wsr/dot_general | solution.py:75
  (4 shorter events, 0.1 us)
Async XLA Ops:
  6.5 85.9 %all-gather.6.cloned.1.call-start = ((), (), s32[]{:S(2)}) async-start(), calls=%async_computation | async-start | bytes 5242880 | tf_op jit(solution)/shard_map/all_gather | solution.py:38
  8.8 189.7 %all-gather.8.cloned.1.call-start = ((), (), s32[]{:S(2)}) async-start(), calls=%async_computation.1 | async-start | bytes 20971520 | tf_op jit(solution)/shard_map/all_gather | solution.py:44
  92.5 180.4 %all-gather.10.cloned.1.call-start = ((), (), s32[]{:S(2)}) async-start(), calls=%async_computation.2 | async-start | bytes 3932160 | tf_op jit(solution)/shard_map/all_gather | solution.py:36
  93.2 241.8 %all-gather.12.cloned.1.call-start = ((), (), s32[]{:S(2)}) async-start(), calls=%async_computation.3 | async-start | bytes 6684672 | tf_op jit(solution)/shard_map/all_gather | solution.py:71
  198.5 38.6 %copy-start.1 = (bf16[1792,192]{0,1:T(8,128)(2,1)S(1)}, bf16[1792,192]{0,1:T(8,128)(2,1)}, u32[]{:S(2)}) copy-start(bf16[1792,192]{0,1:T(8,128)(2,1)} %param.12) | copy-start | bytes 2064388
  264.2 5.2 %copy-start.2 = (f32[512,3584]{1,0:T(8,128)S(1)}, f32[512,3584]{1,0:T(8,128)}, u32[]{:S(2)}) copy-start(f32[512,3584]{1,0:T(8,128)} %fusion) | copy-start | bytes 22020100
  264.2 6.3 %copy-start.3 = (f32[512,1792]{1,0:T(8,128)S(1)}, f32[512,1792]{1,0:T(8,128)}, u32[]{:S(2)}) copy-start(f32[512,1792]{1,0:T(8,128)} %fusion.3) | copy-start | bytes 11010052
  272.9 6.4 %copy-start = (bf16[8192,192]{0,1:T(8,128)(2,1)S(1)}, bf16[8192,192]{0,1:T(8,128)(2,1)}, u32[]{:S(2)}) copy-start(bf16[8192,192]{0,1:T(8,128)(2,1)} %all-gather.10.cloned.1.call-done) | copy-start | bytes 9437188
Sparse Core Ops, SparseCore 0:
  8.9 83.4 all-gather.5
  94.0 104.4 all-gather.7
  200.1 28.5 all-gather.9
  273.0 61.9 all-gather.11
